TPU v7x, 32 devices: a whole 2x2x4 slice. The times are simulated.
32 devices in a mesh: rep: 4 (over y, x), shard: 8 (over z, core).
Axes of the slice: x: 2, y: 2, z: 4, core: 2. Of those that a mesh axis runs over, the one named last changes fastest.
Arguments:
- tokens: bfloat16 [8192, 1024], P(('rep', 'shard')), may hold values from -6 to 6
- cotangent: bfloat16 [8192, 1024], P(('rep', 'shard')), may hold values from -6 to 6
- positions: int32 [8192], P(('rep', 'shard')), may hold values from 0 to 255, as said below
- counts: int32 [32], P(('rep', 'shard')), may hold values from 128 to 256, as said below
- attn_weight: bfloat16 [1024, 3072], P('shard'), may hold values from -0.75 to 0.75
- ffn_weight: bfloat16 [4608, 3, 1024], P('shard'), may hold values from -0.1875 to 0.1875
- gains: bfloat16 [2, 1024], P(None, 'shard'), may hold values from 0.099609375 to 1.8984375
- qk_gains: bfloat16 [2, 64], P(None, 'shard'), as said below
Outputs:
- output: bfloat16 [8192, 1024], P(('rep', 'shard'))
- grad_input: bfloat16 [8192, 1024], P(('rep', 'shard'))
- grad_attn: float32 [1024, 3072], P('shard')
- grad_ffn: float32 [4608, 3, 1024], P('shard')
- grad_gains: float32 [2, 1024], P(None, 'shard')
- grad_qk: float32 [2, 64], P(None, 'shard')
Inputs may be any that keep to these rules, and one draw needn't show every extreme that they name: `counts`: one device holds 256 real tokens and another 128 in every draw. `positions`: sequences lie whole inside one device's block of 256 slots, one after another; slots at or past the block's count hold 0. `qk_gains`: positive scales.
All inputs are finite; a program needn't handle non-finite values.
Results may differ from a plain program's by a relative error of at most 0.018.
Values may be sent and summed in bfloat16 or wider, within the bound.
A program may use at most 320 MiB of HBM per device.

v0:
```python
import jax
import jax.numpy as jnp
from jax import lax
from jax.sharding import PartitionSpec as P

QUERY_HEADS = 16
KEY_VALUE_HEADS = 8
HEAD_WIDTH = 64
QUERY_FEATURES = 1024
KEY_FEATURES = 512
EPS = 1e-05
THETA = 1000000.0


def rope_tables(positions, head_size):
    half = head_size // 2
    freq = THETA ** (-2.0 * jnp.arange(half, dtype=jnp.float32) / head_size)
    angle = positions.astype(jnp.float32)[:, None] * freq[None, :]
    return (jnp.cos(angle), jnp.sin(angle))


def apply_rotation(vectors, cosine_table, sine_table, sign):
    half = vectors.shape[-1] // 2
    upper = vectors[..., :half]
    lower = vectors[..., half:]
    cos_b = cosine_table[:, None, :]
    sin_b = sine_table[:, None, :] * sign
    return jnp.concatenate([upper * cos_b - lower * sin_b, lower * cos_b + upper * sin_b], axis=-1)


def rms_back(grad_normed, unit, inverse, gain):
    inner = grad_normed * gain
    return inverse * (inner - unit * jnp.mean(inner * unit, axis=-1, keepdims=True))


def times_trans(left, right):
    return lax.dot_general(
        left, right, (((1,), (1,)), ((), ())), preferred_element_type=jnp.float32
    )


def trans_times(left, right):
    return lax.dot_general(
        left, right, (((0,), (0,)), ((), ())), preferred_element_type=jnp.float32
    )


def local(tokens, cotangent, positions, counts, attn_weight, ffn_weight, gains, qk_gains):
    token_rows = tokens.shape[0]
    width = QUERY_FEATURES + 2 * KEY_FEATURES
    replica_group = QUERY_HEADS // KEY_VALUE_HEADS
    scale = HEAD_WIDTH ** (-0.5)
    full_attn, full_gains, full_qk = (
        lax.all_gather(attn_weight, "shard", axis=0, tiled=True),
        lax.all_gather(gains, "shard", axis=1, tiled=True),
        lax.all_gather(qk_gains, "shard", axis=1, tiled=True),
    )
    index = jnp.arange(token_rows, dtype=jnp.int32)
    valid = (index < counts[0]).astype(jnp.float32)[:, None]
    allowed = (index[None, :] <= index[:, None]) & (index[None, :] >= (index - positions)[:, None])
    gain_one = full_gains[0].astype(jnp.float32)
    gain_two = full_gains[1].astype(jnp.float32)
    query_gain = full_qk[0].astype(jnp.float32)
    k_gain = full_qk[1].astype(jnp.float32)
    wide = tokens.astype(jnp.float32)
    inv_one = lax.rsqrt(jnp.mean(wide * wide, axis=-1, keepdims=True) + EPS)
    unit_one = wide * inv_one
    normed_one = (unit_one * gain_one).astype(jnp.bfloat16)
    projected_output = jnp.dot(normed_one, full_attn[:, :width], preferred_element_type=jnp.float32)
    query = projected_output[:, :QUERY_FEATURES].reshape(token_rows, QUERY_HEADS, HEAD_WIDTH)
    key_rows = projected_output[:, QUERY_FEATURES : QUERY_FEATURES + KEY_FEATURES].reshape(
        token_rows, KEY_VALUE_HEADS, HEAD_WIDTH
    )
    value_rows = (
        projected_output[:, QUERY_FEATURES + KEY_FEATURES :]
        .reshape(token_rows, KEY_VALUE_HEADS, HEAD_WIDTH)
        .astype(jnp.bfloat16)
    )
    q_inv = lax.rsqrt(jnp.mean(query * query, axis=-1, keepdims=True) + EPS)
    query_unit = query * q_inv
    k_inv = lax.rsqrt(jnp.mean(key_rows * key_rows, axis=-1, keepdims=True) + EPS)
    k_unit = key_rows * k_inv
    cosine_table, sine_table = rope_tables(positions, HEAD_WIDTH)
    query_rotated = (
        apply_rotation(query_unit * query_gain, cosine_table, sine_table, 1.0)
        .astype(jnp.bfloat16)
        .reshape(token_rows, KEY_VALUE_HEADS, replica_group, HEAD_WIDTH)
    )
    key_r = apply_rotation(k_unit * k_gain, cosine_table, sine_table, 1.0).astype(jnp.bfloat16)
    scores = (
        jnp.einsum("qhgd,khd->hgqk", query_rotated, key_r, preferred_element_type=jnp.float32)
        * scale
    )
    masked = jnp.where(allowed, scores, -1e30)
    top = jnp.max(masked, axis=-1, keepdims=True)
    lse = top + jnp.log(jnp.sum(jnp.exp(masked - top), axis=-1, keepdims=True))
    probs = jnp.exp(masked - lse).astype(jnp.bfloat16)
    attended = jnp.einsum(
        "hgqk,khd->qhgd", probs, value_rows, preferred_element_type=jnp.float32
    ).astype(jnp.bfloat16)
    attended_flat = attended.reshape(token_rows, QUERY_FEATURES)
    mid = wide + times_trans(attended_flat, full_attn[:, width:])
    inv_two = lax.rsqrt(jnp.mean(mid * mid, axis=-1, keepdims=True) + EPS)
    unit_two = mid * inv_two
    normed_two = (unit_two * gain_two).astype(jnp.bfloat16)
    piece = lax.all_gather(ffn_weight, "shard", axis=0, tiled=True)
    gate = times_trans(normed_two, piece[:, 0, :])
    up_proj = times_trans(normed_two, piece[:, 1, :])
    hidden_piece = (gate * jax.nn.sigmoid(gate) * up_proj).astype(jnp.bfloat16)
    total = jnp.dot(hidden_piece, piece[:, 2, :], preferred_element_type=jnp.float32)
    gate_all = gate
    up_all = up_proj
    result = ((mid + total) * valid).astype(jnp.bfloat16)
    cot = (cotangent.astype(jnp.float32) * valid).astype(jnp.bfloat16)
    piece = lax.all_gather(ffn_weight, "shard", axis=0, tiled=True)
    gate = gate_all
    up_proj = up_all
    sig = jax.nn.sigmoid(gate)
    d_hidden = times_trans(cot, piece[:, 2, :])
    d_gate = (d_hidden * up_proj * sig * (1.0 + gate * (1.0 - sig))).astype(jnp.bfloat16)
    d_up = (d_hidden * gate * sig).astype(jnp.bfloat16)
    d_normed = jnp.dot(d_gate, piece[:, 0, :], preferred_element_type=jnp.float32) + jnp.dot(
        d_up, piece[:, 1, :], preferred_element_type=jnp.float32
    )
    grad_ffn = lax.psum_scatter(
        jnp.stack(
            [
                trans_times(d_gate, normed_two),
                trans_times(d_up, normed_two),
                trans_times(hidden_piece, cot),
            ],
            axis=1,
        ).astype(jnp.bfloat16),
        "shard",
        scatter_dimension=0,
        tiled=True,
    ).astype(jnp.float32)
    grad_two = jnp.sum(d_normed * unit_two, axis=0)
    d_mid = cot.astype(jnp.float32) + rms_back(d_normed, unit_two, inv_two, gain_two)
    d_mid_b = d_mid.astype(jnp.bfloat16)
    back_attn = lax.all_gather(attn_weight, "shard", axis=0, tiled=True)
    attended_gradient = jnp.dot(
        d_mid_b, back_attn[:, width:], preferred_element_type=jnp.float32
    ).astype(jnp.bfloat16)
    attention_gradient = attended_gradient.reshape(
        token_rows, KEY_VALUE_HEADS, replica_group, HEAD_WIDTH
    )
    scores_again = (
        jnp.einsum("qhgd,khd->hgqk", query_rotated, key_r, preferred_element_type=jnp.float32)
        * scale
    )
    probs_wide = jnp.exp(jnp.where(allowed, scores_again, -1e30) - lse)
    d_probs = jnp.einsum(
        "qhgd,khd->hgqk", attention_gradient, value_rows, preferred_element_type=jnp.float32
    )
    delta = jnp.sum(attention_gradient.astype(jnp.float32) * attended.astype(jnp.float32), axis=-1)
    delta = jnp.transpose(delta, (1, 2, 0))[..., None]
    d_scores = (probs_wide * (d_probs - delta) * scale).astype(jnp.bfloat16)
    d_query_r = jnp.einsum(
        "hgqk,khd->qhgd", d_scores, key_r, preferred_element_type=jnp.float32
    ).reshape(token_rows, QUERY_HEADS, HEAD_WIDTH)
    d_key_r = jnp.einsum(
        "hgqk,qhgd->khd", d_scores, query_rotated, preferred_element_type=jnp.float32
    )
    d_value = jnp.einsum(
        "hgqk,qhgd->khd", probs, attention_gradient, preferred_element_type=jnp.float32
    )
    d_q_scaled = apply_rotation(d_query_r, cosine_table, sine_table, -1.0)
    d_k_scaled = apply_rotation(d_key_r, cosine_table, sine_table, -1.0)
    grad_q = jnp.sum(d_q_scaled * query_unit, axis=(0, 1))
    grad_k = jnp.sum(d_k_scaled * k_unit, axis=(0, 1))
    d_query = rms_back(d_q_scaled, query_unit, q_inv, query_gain)
    d_key = rms_back(d_k_scaled, k_unit, k_inv, k_gain)
    d_projected = jnp.concatenate(
        [
            d_query.reshape(token_rows, QUERY_FEATURES),
            d_key.reshape(token_rows, KEY_FEATURES),
            d_value.reshape(token_rows, KEY_FEATURES),
        ],
        axis=1,
    ).astype(jnp.bfloat16)
    d_normed_one = times_trans(d_projected, back_attn[:, :width])
    grad_one = jnp.sum(d_normed_one * unit_one, axis=0)
    grad_input = (d_mid + rms_back(d_normed_one, unit_one, inv_one, gain_one)).astype(jnp.bfloat16)
    grad_attn = lax.psum_scatter(
        jnp.concatenate(
            [trans_times(normed_one, d_projected), trans_times(d_mid_b, attended_flat)], axis=1
        ).astype(jnp.bfloat16),
        "shard",
        scatter_dimension=0,
        tiled=True,
    ).astype(jnp.float32)
    grad_gains, grad_qk = (
        lax.psum_scatter(jnp.stack([grad_one, grad_two]), "shard", scatter_dimension=1, tiled=True),
        lax.psum_scatter(jnp.stack([grad_q, grad_k]), "shard", scatter_dimension=1, tiled=True),
    )
    grad_attn, grad_ffn, grad_gains, grad_qk = (
        lax.psum(grad_attn.astype(jnp.bfloat16), "rep").astype(jnp.float32),
        lax.psum(grad_ffn.astype(jnp.bfloat16), "rep").astype(jnp.float32),
        lax.psum(grad_gains.astype(jnp.bfloat16), "rep").astype(jnp.float32),
        lax.psum(grad_qk.astype(jnp.bfloat16), "rep").astype(jnp.float32),
    )
    return (result, grad_input, grad_attn, grad_ffn, grad_gains, grad_qk)


def solution(mesh):
    in_specs = (
        P(("rep", "shard"), None),
        P(("rep", "shard"), None),
        P(("rep", "shard")),
        P(("rep", "shard")),
        P("shard", None),
        P("shard", None, None),
        P(None, "shard"),
        P(None, "shard"),
    )
    out_specs = (
        P(("rep", "shard"), None),
        P(("rep", "shard"), None),
        P("shard", None),
        P("shard", None, None),
        P(None, "shard"),
        P(None, "shard"),
    )
    return jax.shard_map(local, mesh=mesh, in_specs=in_specs, out_specs=out_specs, check_vma=False)
```

profile of v0, /device:TPU:0, one launch (start us, length us, event | category | flops | bytes accessed | tf_op | source)
XLA Modules:
  0.0 899.5 jit_solution(8453053964591804986)
XLA Ops:
  8.7 13.5 %all-gather = bf16[8,8,2]{1,2,0:T(2,128)(2,1)S(1)} all-gather(bf16[1,8,2]{1,2,0:T(2,128)(2,1)S(1)} %bitcast.186), channel_id=1, replica_groups=mesh['rep'=4,'shard'=8] {'shard'}, dimensions={0}, use_global_device_ids=true | all-gather | bytes 288 | tf_op jit(solution)/shard_map/all_gather | solution.py:56
  23.1 9.1 %all_gather.14 = bf16[2,1024]{1,0:T(2,128)(2,1)S(1)} all-gather(bf16[2,128]{1,0:T(2,128)(2,1)S(1)} %copy-done.45), channel_id=1, replica_groups=mesh['rep'=4,'shard'=8] {'shard'}, dimensions={1}, use_global_device_ids=true | all-gather | bytes 4608 | tf_op jit(solution)/shard_map/all_gather | solution.py:55
  33.9 43.2 %all-gather.4.cloned.1.call-done = bf16[1024,3072]{1,0:T(8,128)(2,1)} async-done(((bf16[128,3072]{1,0:T(8,128)(2,1)}), bf16[1024,3072]{1,0:T(8,128)(2,1)}) %all-gather.4.cloned.1.call-update) | async-done | bytes 6291472 | tf_op jit(solution)/shard_map/all_gather | solution.py:54
  77.1 3.5 fusion.15
  90.6 3.1 multiply_reduce_fusion.5
  94.8 228.2 %all-gather.6.cloned.1.call-done = bf16[4608,3,1024]{2,0,1:T(8,128)(2,1)} async-done(((bf16[576,3,1024]{2,0,1:T(8,128)(2,1)}), bf16[4608,3,1024]{2,0,1:T(8,128)(2,1)}) %all-gather.6.cloned.1.call-update) | async-done | bytes 28311568 | tf_op jit(solution)/shard_map/all_gather | solution.py:106
  323.0 5.2 fusion.1
  328.3 8.6 fusion.3
  336.8 9.0 multiply_convert_fusion
  345.8 6.9 fusion
  352.8 6.2 multiply_reduce_fusion.1
  359.4 3.1 fusion.32
  365.9 4.3 fusion.35
  383.7 2.7 copy.84
  387.5 2.6 copy.86
  391.7 2.4 multiply_reduce_fusion
  396.3 3.3 pad_maximum_fusion.1
  400.6 6.9 fusion.7
  407.4 5.1 fusion.6
  412.6 5.2 fusion.8
  417.8 19.8 %pad_maximum_fusion = bf16[4608,3,1024]{2,0,1:T(8,128)(2,1)} fusion(bf16[4608,1,1024]{2,0,1:T(8,128)(2,1)} %fusion.8, bf16[4608,1,1024]{2,0,1:T(8,128)(2,1)} %fusion.7, bf16[4608,1,1024]{2,0,1:T(8,128)(2,1)} %fusion.6), kind=kLoop, calls=%fused_computation | loop fusion | flops 28311552 | bytes 56623104 | tf_op jit(solution)/shard_map/stack | solution.py:126
  438.8 4.6 fusion.42
  444.6 23.0 %reduce-scatter.7.cloned.1.call-done = bf16[128,3072]{1,0:T(8,128)(2,1)} async-done(((bf16[1024,3072]{1,0:T(8,128)(2,1)}), bf16[128,3072]{1,0:T(8,128)(2,1)}) %reduce-scatter.7.cloned.1.call-update) | async-done | bytes 786448 | tf_op jit(solution)/shard_map/reduce_scatter | solution.py:185
  467.6 277.4 %reduce-scatter.9.cloned.1.call-done = bf16[576,3,1024]{2,0,1:T(8,128)(2,1)} async-done(((bf16[4608,3,1024]{2,0,1:T(8,128)(2,1)}), bf16[576,3,1024]{2,0,1:T(8,128)(2,1)}) %reduce-scatter.9.cloned.1.call-update) | async-done | bytes 3538960 | tf_op jit(solution)/shard_map/reduce_scatter | solution.py:125
  746.5 13.7 %all-reduce = bf16[2,64]{1,0:T(2,128)(2,1)S(1)} all-reduce(f32[2,64]{1,0:T(2,128)S(1)} %pad_maximum_fusion.11), channel_id=5, replica_groups=mesh['rep'=4,'shard'=8] {'shard'}, use_global_device_ids=true, to_apply=%region_23.24.clone | all-reduce | flops 128 | bytes 768
  760.3 2.3 fusion.41
  762.6 7.9 fusion.31
  770.5 6.6 reduce-scatter.11.cloned.1.call-done
  778.0 9.9 %all-reduce.1 = (bf16[2,128]{1,0:T(2,128)(2,1)S(1)}, bf16[2,8]{1,0:T(2,128)(2,1)S(1)}) all-reduce(bf16[2,128]{1,0:T(2,128)(2,1)S(1)} %copy.108, bf16[2,8]{1,0:T(2,128)(2,1)S(1)} %dynamic-slice_convert_fusion), channel_id=1, replica_groups=mesh['rep'=4,'shard'=8] {'rep'}, use_global_device_ids=true, to_apply=%region_18.19 | all-reduce | flops 272 | bytes 1088 | tf_op jit(solution)/shard_map/psum | solution.py:200
  789.0 95.4 %all-reduce.5.cloned.1.call-done = (bf16[128,3072]{1,0:T(8,128)(2,1)}, bf16[576,3,1024]{2,0,1:T(8,128)(2,1)}) async-done(((bf16[128,3072]{1,0:T(8,128)(2,1)}, bf16[576,3,1024]{2,0,1:T(8,128)(2,1)}), (bf16[128,3072]{1,0:T(8,128)(2,1)}, bf16[576,3,1024]{2,0,1:T(8,128)(2,1)})) %all-reduce.5.cloned.1.call-update) | async-done | bytes 4325392 | tf_op jit(solution)/shard_map/psum | solution.py:198
  884.4 2.4 convert_element_type.149
  886.8 5.8 convert_element_type.150
  (179 shorter events, 42.7 us)
Async XLA Ops:
  7.2 16.0 %copy-start.45 = (bf16[2,128]{1,0:T(2,128)(2,1)S(1)}, bf16[2,128]{1,0:T(2,128)(2,1)}, u32[]{:S(2)}) copy-start(bf16[2,128]{1,0:T(2,128)(2,1)} %param.14) | copy-start | bytes 1540
  7.2 25.6 %copy-start.15 = (bf16[256,1024]{1,0:T(8,128)(2,1)S(1)}, bf16[256,1024]{1,0:T(8,128)(2,1)}, u32[]{:S(2)}) copy-start(bf16[256,1024]{1,0:T(8,128)(2,1)} %param.8) | copy-start | bytes 1572868
  7.2 25.8 %copy-start.43 = (s32[256]{0:T(256)S(1)}, s32[256]{0:T(256)}, u32[]{:S(2)}) copy-start(s32[256]{0:T(256)} %param.10) | copy-start | bytes 3076
  7.2 69.9 %all-gather.4.cloned.1.call-start = ((), (), s32[]{:S(2)}) async-start(), calls=%async_computation.3 | async-start | bytes 7077888 | tf_op jit(solution)/shard_map/all_gather | solution.py:54
  7.9 315.1 %all-gather.6.cloned.1.call-start = ((), (), s32[]{:S(2)}) async-start(), calls=%async_computation.4 | async-start | bytes 31850496 | tf_op jit(solution)/shard_map/all_gather | solution.py:106
  8.7 458.9 %reduce-scatter.7.cloned.1.call-start = ((), (), s32[]{:S(2)}) async-start(), calls=%async_computation.5 | async-start | bytes 7077888 | tf_op jit(solution)/shard_map/reduce_scatter | solution.py:185
  33.0 47.6 %copy-start.38 = (f32[256]{0:T(256)}, f32[256]{0:T(256)S(1)}, u32[]{:S(2)}) copy-start(f32[256]{0:T(256)S(1)} %add_rsqrt_fusion.3) | copy-start | bytes 3076
  94.8 233.4 %copy-start.3 = (bf16[256,1024]{1,0:T(8,128)(2,1)}, bf16[256,1024]{1,0:T(8,128)(2,1)S(1)}, u32[]{:S(2)}) copy-start(bf16[256,1024]{1,0:T(8,128)(2,1)S(1)} %multiply_convert_fusion.5) | copy-start | bytes 1572868
  328.2 8.6 copy-start.19
  328.3 8.6 copy-start.41
  345.8 6.9 copy-start.10
  345.8 6.9 copy-start.12
  345.8 6.9 copy-start.6
  359.0 7.0 copy-start.37
  364.5 5.7 copy-start.9
  364.5 5.7 copy-start.14
  364.5 5.7 copy-start.30
  364.6 5.7 copy-start.34
  383.7 6.3 copy-start.2
  387.5 7.4 copy-start.39
  390.1 4.8 copy-start.17
  390.1 4.8 copy-start.31
  399.5 345.5 %reduce-scatter.9.cloned.1.call-start = ((), (), s32[]{:S(2)}) async-start(), calls=%async_computation.6 | async-start | bytes 31850496 | tf_op jit(solution)/shard_map/reduce_scatter | solution.py:125
  400.6 6.9 copy-start.11
  407.4 5.2 copy-start.13
  407.4 5.2 copy-start.20
  407.4 5.2 copy-start.42
  437.6 5.8 copy-start.40
  437.6 339.5 %reduce-scatter.11.cloned.1.call-start = ((), (), s32[]{:S(2)}) async-start(), calls=%async_computation.7 | async-start | bytes 589824
  443.4 301.6 %copy-start.46 = (u32[32]{0:T(128)S(1)}, u32[32]{0:T(128)}, u32[]{:S(2)}) copy-start(u32[32]{0:T(128)} %constant.39) | copy-start | bytes 388
  443.4 319.2 %copy-start.7 = (f32[256,1024]{1,0:T(8,128)S(1)}, f32[256,1024]{1,0:T(8,128)}, u32[]{:S(2)}) copy-start(f32[256,1024]{1,0:T(8,128)} %copy-done.5) | copy-start | bytes 3145732
  444.5 439.9 %all-reduce.5.cloned.1.call-start = ((), (), s32[]{:S(2)}) async-start(), calls=%async_computation.8 | async-start | bytes 8650752 | tf_op jit(solution)/shard_map/psum | solution.py:198
  (21 other events, 40.0 us)
Sparse Core Ops, SparseCore 0:
  9.7 67.3 all-gather.3
  78.7 244.2 all-gather.5
  399.7 67.8 reduce-scatter.6
  469.8 275.1 reduce-scatter.8
  747.1 29.9 reduce-scatter.10
  780.5 103.8 all-reduce.4
where the time goes:
time: 900 us; the launch traced here: 899 us
  waiting for transfers between devices  675 us (75%)
  matrix products  90.3 us (10%)
  other arithmetic  47.9 us (5%)
  blocking collectives  46.2 us (5%)
  local copies, waits for them, and re-layouts  23.5 us (3%)
  between operations  16.1 us (2%)
    reduce_scatter x1, waiting for transfers between devices, local(): lax.psum_scatter(jnp.stack([trans_times(d_gate, normed_two), trans_times(...  277 us
    all_gather x1, waiting for transfers between devices, local(): piece = lax.all_gather(ffn_weight, 'shard', axis=0, tiled=True)  228 us
    psum x1, waiting for transfers between devices, local(): lax.psum(grad_attn.astype(jnp.bfloat16), 'rep').astype(jnp.float32)  95.4 us
    all_gather x1, waiting for transfers between devices, local(): lax.all_gather(attn_weight, 'shard', axis=0, tiled=True)  43.2 us
    dot_general x5, matrix products, times_trans(): lax.dot_general(left, right, (((1,), (1,)), ((), ())), preferred_element_...  30.4 us
    reduce_scatter x1, waiting for transfers between devices, local(): lax.psum_scatter(jnp.concatenate([trans_times(normed_one, d_projected), t...  23 us
    dot_general x5, matrix products, trans_times(): lax.dot_general(left, right, (((0,), (0,)), ((), ())), preferred_element_...  20.6 us
    another operation x1, other arithmetic, local(): jnp.stack([trans_times(d_gate, normed_two), trans_times(d_up, normed_two)...  19.8 us
  transfers between devices with their start and end apart: 6, of which 6 were waited for; matrix products, arithmetic and copies ran while one was open for 8% of the time, Pallas kernels for 0%

commit v1 on v0

--- a/solution.py
+++ b/solution.py
@@ -195,7 +195,9 @@
         lax.psum_scatter(jnp.stack([grad_q, grad_k]), "shard", scatter_dimension=1, tiled=True),
     )
     grad_attn, grad_ffn, grad_gains, grad_qk = (
-        lax.psum(grad_attn.astype(jnp.bfloat16), "rep").astype(jnp.float32),
+        jnp.sum(lax.all_gather(grad_attn.astype(jnp.bfloat16), axis_name="rep"), axis=0).astype(
+            jnp.float32
+        ),
         lax.psum(grad_ffn.astype(jnp.bfloat16), "rep").astype(jnp.float32),
         lax.psum(grad_gains.astype(jnp.bfloat16), "rep").astype(jnp.float32),
         lax.psum(grad_qk.astype(jnp.bfloat16), "rep").astype(jnp.float32),

time: 900 us -> 931 us (1.034)
  waiting for transfers between devices: 675 us -> 704 us
    all_gather x0 -> x1, waiting for transfers between devices: none -> 31.7 us  [local(): lax.all_gather(grad_attn.astype(jnp.bfloat16), axis_name='rep')]
  transfers between devices with their start and end apart: 6 -> 7, of which waited for: 6 -> 7; matrix products, arithmetic and copies ran while one was open for 8% -> 8% of each run, Pallas kernels for 0% -> 0%
where the time goes in v1:
time: 931 us; the launch traced here: 930 us
  waiting for transfers between devices  704 us (76%)
  matrix products  90.4 us (10%)
  other arithmetic  49.3 us (5%)
  blocking collectives  46.3 us (5%)
  local copies, waits for them, and re-layouts  23.5 us (3%)
  between operations  16.1 us (2%)
    reduce_scatter x1, waiting for transfers between devices, local(): lax.psum_scatter(jnp.stack([trans_times(d_gate, normed_two), trans_times(...  277 us
    all_gather x1, waiting for transfers between devices, local(): piece = lax.all_gather(ffn_weight, 'shard', axis=0, tiled=True)  228 us
    psum x1, waiting for transfers between devices, local(): lax.psum(grad_ffn.astype(jnp.bfloat16), 'rep').astype(jnp.float32)  92.9 us
    all_gather x1, waiting for transfers between devices, local(): lax.all_gather(attn_weight, 'shard', axis=0, tiled=True)  43.2 us
    all_gather x1, waiting for transfers between devices, local(): lax.all_gather(grad_attn.astype(jnp.bfloat16), axis_name='rep')  31.7 us
    dot_general x5, matrix products, times_trans(): lax.dot_general(left, right, (((1,), (1,)), ((), ())), preferred_element_...  30.5 us
    reduce_scatter x1, waiting for transfers between devices, local(): lax.psum_scatter(jnp.concatenate([trans_times(normed_one, d_projected), t...  23 us
    dot_general x5, matrix products, trans_times(): lax.dot_general(left, right, (((0,), (0,)), ((), ())), preferred_element_...  20.6 us
  transfers between devices with their start and end apart: 7, of which 7 were waited for; matrix products, arithmetic and copies ran while one was open for 8% of the time, Pallas kernels for 0%

profile of v1, /device:TPU:0, one launch (start us, length us, event | category | flops | bytes accessed | tf_op | source)
XLA Modules:
  0.0 930.3 jit_solution(18243505765342746141)
XLA Ops:
  8.7 13.5 %all-gather.1 = bf16[8,8,2]{1,2,0:T(2,128)(2,1)S(1)} all-gather(bf16[1,8,2]{1,2,0:T(2,128)(2,1)S(1)} %bitcast.188), channel_id=1, replica_groups=mesh['rep'=4,'shard'=8] {'shard'}, dimensions={0}, use_global_device_ids=true | all-gather | bytes 288 | tf_op jit(solution)/shard_map/all_gather | solution.py:56
  23.1 9.1 all_gather.20
  33.9 43.2 %all-gather.6.cloned.1.call-done = bf16[1024,3072]{1,0:T(8,128)(2,1)} async-done(((bf16[128,3072]{1,0:T(8,128)(2,1)}), bf16[1024,3072]{1,0:T(8,128)(2,1)}) %all-gather.6.cloned.1.call-update) | async-done | bytes 6291472 | tf_op jit(solution)/shard_map/all_gather | solution.py:54
  77.1 3.5 fusion.15
  90.6 3.1 multiply_reduce_fusion.5
  94.8 228.2 %all-gather.8.cloned.1.call-done = bf16[4608,3,1024]{2,0,1:T(8,128)(2,1)} async-done(((bf16[576,3,1024]{2,0,1:T(8,128)(2,1)}), bf16[4608,3,1024]{2,0,1:T(8,128)(2,1)}) %all-gather.8.cloned.1.call-update) | async-done | bytes 28311568 | tf_op jit(solution)/shard_map/all_gather | solution.py:106
  323.0 5.2 fusion.1
  328.3 8.6 fusion.3
  336.8 9.0 multiply_convert_fusion
  345.8 6.9 fusion
  352.8 6.2 multiply_reduce_fusion.1
  359.4 3.1 fusion.32
  366.0 4.4 fusion.35
  383.7 2.7 copy.84
  387.5 2.6 copy.86
  391.7 2.4 multiply_reduce_fusion
  396.3 3.3 pad_maximum_fusion.1
  400.6 6.9 fusion.7
  407.5 5.1 fusion.6
  412.6 5.2 fusion.8
  417.8 19.8 %pad_maximum_fusion = bf16[4608,3,1024]{2,0,1:T(8,128)(2,1)} fusion(bf16[4608,1,1024]{2,0,1:T(8,128)(2,1)} %fusion.8, bf16[4608,1,1024]{2,0,1:T(8,128)(2,1)} %fusion.7, bf16[4608,1,1024]{2,0,1:T(8,128)(2,1)} %fusion.6), kind=kLoop, calls=%fused_computation | loop fusion | flops 28311552 | bytes 56623104 | tf_op jit(solution)/shard_map/stack | solution.py:126
  438.9 4.6 fusion.42
  444.7 23.0 %reduce-scatter.7.cloned.1.call-done = bf16[128,3072]{1,0:T(8,128)(2,1)} async-done(((bf16[1024,3072]{1,0:T(8,128)(2,1)}), bf16[128,3072]{1,0:T(8,128)(2,1)}) %reduce-scatter.7.cloned.1.call-update) | async-done | bytes 786448 | tf_op jit(solution)/shard_map/reduce_scatter | solution.py:185
  467.7 277.3 %reduce-scatter.9.cloned.1.call-done = bf16[576,3,1024]{2,0,1:T(8,128)(2,1)} async-done(((bf16[4608,3,1024]{2,0,1:T(8,128)(2,1)}), bf16[576,3,1024]{2,0,1:T(8,128)(2,1)}) %reduce-scatter.9.cloned.1.call-update) | async-done | bytes 3538960 | tf_op jit(solution)/shard_map/reduce_scatter | solution.py:125
  746.5 13.7 %all-reduce = bf16[2,64]{1,0:T(2,128)(2,1)S(1)} all-reduce(f32[2,64]{1,0:T(2,128)S(1)} %pad_maximum_fusion.11), channel_id=6, replica_groups=mesh['rep'=4,'shard'=8] {'shard'}, use_global_device_ids=true, to_apply=%region_23.24.clone | all-reduce | flops 128 | bytes 768
  762.6 7.9 fusion.31
  770.5 6.6 reduce-scatter.11.cloned.1.call-done
  778.0 10.0 %all-reduce.1 = (bf16[2,128]{1,0:T(2,128)(2,1)S(1)}, bf16[2,8]{1,0:T(2,128)(2,1)S(1)}) all-reduce(bf16[2,128]{1,0:T(2,128)(2,1)S(1)} %copy.108, bf16[2,8]{1,0:T(2,128)(2,1)S(1)} %dynamic-slice_convert_fusion), channel_id=1, replica_groups=mesh['rep'=4,'shard'=8] {'rep'}, use_global_device_ids=true, to_apply=%region_18.19 | all-reduce | flops 272 | bytes 1088 | tf_op jit(solution)/shard_map/psum | solution.py:202
  789.1 31.7 %all-gather.10.cloned.1.call-done = bf16[512,3072]{1,0:T(8,128)(2,1)} async-done(((bf16[128,3072]{1,0:T(8,128)(2,1)}), bf16[512,3072]{1,0:T(8,128)(2,1)}) %all-gather.10.cloned.1.call-update) | async-done | bytes 3145744 | tf_op jit(solution)/shard_map/all_gather | solution.py:198
  820.9 2.5 reduce_sum.162
  824.7 92.9 %all-reduce.4.cloned.1.call-done = bf16[576,3,1024]{2,0,1:T(8,128)(2,1)} async-done(((bf16[576,3,1024]{2,0,1:T(8,128)(2,1)}), bf16[576,3,1024]{2,0,1:T(8,128)(2,1)}) %all-reduce.4.cloned.1.call-update) | async-done | bytes 3538960 | tf_op jit(solution)/shard_map/psum | solution.py:201
  917.6 5.8 convert_element_type.152
  (183 shorter events, 46.3 us)
Async XLA Ops:
  7.2 16.0 %copy-start.45 = (bf16[2,128]{1,0:T(2,128)(2,1)S(1)}, bf16[2,128]{1,0:T(2,128)(2,1)}, u32[]{:S(2)}) copy-start(bf16[2,128]{1,0:T(2,128)(2,1)} %param.14) | copy-start | bytes 1540
  7.2 25.6 %copy-start.15 = (bf16[256,1024]{1,0:T(8,128)(2,1)S(1)}, bf16[256,1024]{1,0:T(8,128)(2,1)}, u32[]{:S(2)}) copy-start(bf16[256,1024]{1,0:T(8,128)(2,1)} %param.8) | copy-start | bytes 1572868
  7.2 25.8 %copy-start.43 = (s32[256]{0:T(256)S(1)}, s32[256]{0:T(256)}, u32[]{:S(2)}) copy-start(s32[256]{0:T(256)} %param.10) | copy-start | bytes 3076
  7.2 69.9 %all-gather.6.cloned.1.call-start = ((), (), s32[]{:S(2)}) async-start(), calls=%async_computation.3 | async-start | bytes 7077888 | tf_op jit(solution)/shard_map/all_gather | solution.py:54
  7.9 315.1 %all-gather.8.cloned.1.call-start = ((), (), s32[]{:S(2)}) async-start(), calls=%async_computation.4 | async-start | bytes 31850496 | tf_op jit(solution)/shard_map/all_gather | solution.py:106
  8.7 458.9 %reduce-scatter.7.cloned.1.call-start = ((), (), s32[]{:S(2)}) async-start(), calls=%async_computation.5 | async-start | bytes 7077888 | tf_op jit(solution)/shard_map/reduce_scatter | solution.py:185
  33.0 47.6 %copy-start.38 = (f32[256]{0:T(256)}, f32[256]{0:T(256)S(1)}, u32[]{:S(2)}) copy-start(f32[256]{0:T(256)S(1)} %add_rsqrt_fusion.3) | copy-start | bytes 3076
  94.8 233.4 %copy-start.3 = (bf16[256,1024]{1,0:T(8,128)(2,1)}, bf16[256,1024]{1,0:T(8,128)(2,1)S(1)}, u32[]{:S(2)}) copy-start(bf16[256,1024]{1,0:T(8,128)(2,1)S(1)} %multiply_convert_fusion.5) | copy-start | bytes 1572868
  328.2 8.6 copy-start.19
  328.3 8.6 copy-start.41
  345.8 6.9 copy-start.10
  345.8 6.9 copy-start.12
  345.8 6.9 copy-start.6
  359.0 7.0 copy-start.37
  364.6 5.8 copy-start.9
  364.6 5.8 copy-start.14
  364.6 5.8 copy-start.30
  364.6 5.8 copy-start.34
  383.7 6.3 copy-start.2
  387.5 7.4 copy-start.39
  390.1 4.8 copy-start.31
  399.6 345.5 %reduce-scatter.9.cloned.1.call-start = ((), (), s32[]{:S(2)}) async-start(), calls=%async_computation.6 | async-start | bytes 31850496 | tf_op jit(solution)/shard_map/reduce_scatter | solution.py:125
  400.6 6.9 copy-start.11
  407.4 5.1 copy-start.13
  407.4 5.1 copy-start.20
  407.4 5.1 copy-start.42
  437.6 5.9 copy-start.40
  437.7 339.5 %reduce-scatter.11.cloned.1.call-start = ((), (), s32[]{:S(2)}) async-start(), calls=%async_computation.9 | async-start | bytes 589824
  443.5 301.5 %copy-start.46 = (u32[32]{0:T(128)S(1)}, u32[32]{0:T(128)}, u32[]{:S(2)}) copy-start(u32[32]{0:T(128)} %constant.41) | copy-start | bytes 388
  443.5 319.1 %copy-start.7 = (f32[256,1024]{1,0:T(8,128)S(1)}, f32[256,1024]{1,0:T(8,128)}, u32[]{:S(2)}) copy-start(f32[256,1024]{1,0:T(8,128)} %copy-done.5) | copy-start | bytes 3145732
  444.6 376.2 %all-gather.10.cloned.1.call-start = ((), (), s32[]{:S(2)}) async-start(), calls=%async_computation.8 | async-start | bytes 3932160 | tf_op jit(solution)/shard_map/all_gather | solution.py:198
  467.6 449.9 %all-reduce.4.cloned.1.call-start = ((), (), s32[]{:S(2)}) async-start(), calls=%async_computation.7 | async-start | bytes 7077888 | tf_op jit(solution)/shard_map/psum | solution.py:201
  (22 other events, 44.8 us)
Sparse Core Ops, SparseCore 0:
  9.7 67.3 all-gather.5
  78.7 244.2 all-gather.7
  399.7 67.8 reduce-scatter.6
  469.8 275.1 reduce-scatter.8
  747.1 29.9 reduce-scatter.10
  778.8 41.9 all-gather.9
  824.0 93.4 all-reduce.3
